TPU v7x, 32 devices: a whole 2x2x4 slice. The times are simulated.
32 devices in a mesh: mem: 8 (over z, y), lev: 4 (over x, core).
Axes of the slice: x: 2, y: 2, z: 4, core: 2. Of those that a mesh axis runs over, the one named last changes fastest.
Arguments:
- prior_ensemble_stack: float32 [16, 20, 64, 512], P('mem', 'lev'), may hold values from -6 to 6
- vertical_cfl_ratio: float32 [20, 64, 512], P('lev'), may hold values from -0.35 to 0.35
- horizontal_cfl_ratio: float32 [20, 64, 512], P('lev'), may hold values from -0.35 to 0.35
- spreading_coefficient: float32 [20], P('lev'), may hold values from 0.02 to 0.2
- obs_cells: int32 [2, 16], replicated, may hold values from 0 to 32767
- obs_slabs: int32 [2, 16], replicated, may hold values from 0 to 19
- obs_values: float32 [2, 16], replicated, may hold values from -6 to 6
- obs_error: float32 [2, 16], replicated, may hold values from 0.25 to 2
Outputs:
- analysis: float32 [16, 20, 64, 512], P('mem', 'lev')
All inputs are finite; a program needn't handle non-finite values.
Results may differ from a plain program's by a relative error of at most 0.0001.
Values sent between devices are 32-bit elements; how exact they have to be, the bound alone decides.
No kernel may reach another device: no remote copies, remote signals or barrier semaphores. Data moves between devices by JAX's collectives and lax.ppermute only.
A program may use at most 256 MiB of HBM per device.

v0:
```python
import jax
import jax.numpy as jnp
from jax import lax
from jax.sharding import PartitionSpec as P

NX = 512
STEPS = 2
LOC_HALF = 64


def predicted_model_vector(
    ensemble_gridded_values, vertical_cfl_ratio, horizontal_cfl_ratio, spreading_coefficient
):
    diffuse = spreading_coefficient[:, None, None]
    for time_step in range(STEPS):
        widths = [(0, 0)] * (ensemble_gridded_values.ndim - 2) + [(1, 1), (1, 1)]
        padded = jnp.pad(ensemble_gridded_values, widths, mode="edge")
        east_cell = padded[..., 1:-1, 2:]
        west_cell = padded[..., 1:-1, :-2]
        north_cell = padded[..., 2:, 1:-1]
        south_cell = padded[..., :-2, 1:-1]
        ensemble_gridded_values = (
            ensemble_gridded_values
            - 0.5 * vertical_cfl_ratio * (east_cell - west_cell)
            - 0.5 * horizontal_cfl_ratio * (north_cell - south_cell)
            + diffuse
            * (east_cell + west_cell + north_cell + south_cell - 4.0 * ensemble_gridded_values)
        )
    return ensemble_gridded_values


def grid_distance(cells_a, cells_b):
    row_gap = (cells_a[:, None] // NX - cells_b[None, :] // NX).astype(jnp.float32)
    col_gap = (cells_a[:, None] % NX - cells_b[None, :] % NX).astype(jnp.float32)
    return jnp.sqrt(row_gap * row_gap + col_gap * col_gap)


def gaspari_taper(dist):
    scaled = dist / LOC_HALF
    inner_portion = (
        ((-0.25 * scaled + 0.5) * scaled + 0.625) * scaled - 5.0 / 3.0
    ) * scaled * scaled + 1.0
    safe_ratio = jnp.maximum(scaled, 1.0)
    outer_portion = (
        ((((scaled / 12.0 - 0.5) * scaled + 0.625) * scaled + 5.0 / 3.0) * scaled - 5.0) * scaled
        + 4.0
        - 2.0 / (3.0 * safe_ratio)
    )
    return jnp.where(scaled <= 1.0, inner_portion, jnp.where(scaled < 2.0, outer_portion, 0.0))


def obs_space(prior_rows, row_cells, first_row, obs_cell, obs_value, obs_var):
    member_count = prior_rows.shape[1]
    reach_table = gaspari_taper(grid_distance(row_cells, obs_cell))

    def advance_obs(current, position):
        own_row = lax.dynamic_index_in_dim(current, first_row + position, 0, False)
        row_mean = jnp.mean(own_row)
        anomaly = own_row - row_mean
        spread = jnp.sum(anomaly * anomaly) / (member_count - 1) + 1e-06
        error_var = lax.dynamic_index_in_dim(obs_var, position, 0, False)
        seen_value = lax.dynamic_index_in_dim(obs_value, position, 0, False)
        shrink = jnp.sqrt(error_var / (spread + error_var))
        increment = (
            (row_mean * error_var + seen_value * spread) / (spread + error_var)
            - row_mean
            + (shrink - 1.0) * anomaly
        )
        centered = current - jnp.mean(current, axis=1, keepdims=True)
        slopes = jnp.dot(centered, anomaly, precision=lax.Precision.HIGHEST) / (
            (member_count - 1) * spread
        )
        weight = lax.dynamic_index_in_dim(reach_table, position, 1, False)
        current = current + (weight * slopes)[:, None] * increment[None, :]
        return (current, (anomaly, spread, increment))

    positions = jnp.arange(obs_cell.shape[0], dtype=jnp.int32)
    prior_rows, obs_plan = lax.scan(advance_obs, prior_rows, positions)
    return (obs_plan, prior_rows)


def settle(state_rows, obs_plan, cell_loc):
    prior_anoms, spreads, increments = obs_plan
    member_count = state_rows.shape[0]
    centered = state_rows - jnp.mean(state_rows, axis=0, keepdims=True)
    cross_cov = jnp.einsum(
        "km,msc->ksc", prior_anoms, centered, precision=lax.Precision.HIGHEST
    ) / (member_count - 1)
    incr_anom = increments - jnp.mean(increments, axis=1, keepdims=True)
    incr_link = jnp.dot(incr_anom, prior_anoms.T, precision=lax.Precision.HIGHEST) / (
        member_count - 1
    )

    def solve_step(weights, position):
        column = lax.dynamic_index_in_dim(incr_link, position, 1, False)
        summed_total = lax.dynamic_index_in_dim(cross_cov, position, 0, False) + jnp.einsum(
            "j,jsc->sc", column, weights, precision=lax.Precision.HIGHEST
        )
        taper_row = lax.dynamic_index_in_dim(cell_loc, position, 0, False)
        update_row = (
            taper_row[None, :]
            * summed_total
            / lax.dynamic_index_in_dim(spreads, position, 0, False)
        )
        return (lax.dynamic_update_index_in_dim(weights, update_row, position, 0), None)

    positions = jnp.arange(cross_cov.shape[0], dtype=jnp.int32)
    weights, unused = lax.scan(solve_step, jnp.zeros_like(cross_cov), positions)
    return state_rows + jnp.einsum(
        "km,ksc->msc", increments, weights, precision=lax.Precision.HIGHEST
    )


def pick_rows(state_rows, obs_slab, obs_cell, slab_base, cell_base):
    slab_dev = state_rows.shape[1]
    cell_dev = state_rows.shape[2]
    slab_off = obs_slab - slab_base
    cell_off = obs_cell - cell_base
    inside = (slab_off >= 0) & (slab_off < slab_dev) & (cell_off >= 0) & (cell_off < cell_dev)
    taken_rows = state_rows[
        :, jnp.clip(slab_off, 0, slab_dev - 1), jnp.clip(cell_off, 0, cell_dev - 1)
    ]
    return jnp.where(inside[:, None], taken_rows.T, 0.0)


def body(
    prior_ensemble_stack,
    vertical_cfl_ratio,
    horizontal_cfl_ratio,
    spreading_coefficient,
    obs_cells,
    obs_slabs,
    obs_values,
    obs_error,
):
    mem_dev, slab_dev, grid_rows, grid_cols = prior_ensemble_stack.shape
    cell_total = grid_rows * grid_cols
    cell_dev = cell_total // lax.axis_size("mem")
    batch_count = obs_cells.shape[0]
    ensemble_gridded_values = predicted_model_vector(
        prior_ensemble_stack, vertical_cfl_ratio, horizontal_cfl_ratio, spreading_coefficient
    )
    by_cells = ensemble_gridded_values.reshape(mem_dev, slab_dev, cell_total)
    cell_base = lax.axis_index("mem") * cell_dev
    slab_base = lax.axis_index("lev") * slab_dev
    local_cells = cell_base + jnp.arange(cell_dev, dtype=jnp.int32)
    cell_locs = [
        gaspari_taper(grid_distance(obs_cells[batch_no], local_cells))
        for batch_no in range(batch_count)
    ]
    state_rows = lax.all_to_all(by_cells, "mem", split_axis=2, concat_axis=0, tiled=True)
    for batch_no in range(batch_count):
        partial_value = pick_rows(
            state_rows, obs_slabs[batch_no], obs_cells[batch_no], slab_base, cell_base
        )
        prior_rows = lax.psum(partial_value, ("mem", "lev"))
        obs_plan, carried = obs_space(
            prior_rows,
            obs_cells[batch_no],
            0,
            obs_cells[batch_no],
            obs_values[batch_no],
            obs_error[batch_no],
        )
        state_rows = settle(state_rows, obs_plan, cell_locs[batch_no])
    result = lax.all_to_all(state_rows, "mem", split_axis=0, concat_axis=2, tiled=True)
    return result.reshape(prior_ensemble_stack.shape)


def solution(mesh):
    in_specs = (
        P("mem", "lev", None, None),
        P("lev", None, None),
        P("lev", None, None),
        P("lev"),
        P(),
        P(),
        P(),
        P(),
    )
    out_specs = P("mem", "lev", None, None)
    return jax.shard_map(body, mesh=mesh, in_specs=in_specs, out_specs=out_specs, check_vma=False)
```

profile of v0, /device:TPU:0, one launch (start us, length us, event | category | flops | bytes accessed | tf_op | source)
XLA Modules:
  0.0 932.9 jit_solution(16619717677496745712)
XLA Ops:
  2.7 2.2 multiply_add_fusion.5
  5.0 2.2 multiply_add_fusion.4
  7.2 22.3 %copy.76 = f32[2,5,64,512]{1,0,3,2:T(2,128)} copy(f32[2,5,64,512]{3,2,1,0:T(8,128)S(1)} %multiply_add_fusion.4) | data formatting | bytes 2621440 | tf_op jit(solution)/shard_map/reshape | solution.py:143
  29.5 53.2 %reshape.447 = f32[8,1,40960]{2,1,0:T(1,128)} reshape(f32[32768,2,5]{2,1,0:T(2,128)} %bitcast.261) | data formatting | bytes 2621440
  82.7 7.6 all-to-all-start
  92.0 1.6 fusion.55
  93.6 27.9 %all-to-all-done = f32[8,1,40960]{2,1,0:T(1,128)S(1)} async-done(((f32[8,1,40960]{2,1,0:T(1,128)}), f32[8,1,40960]{2,1,0:T(1,128)S(1)}, u32[]{:S(2)}, u32[]{:S(2)}) %all-to-all-start) | async-done | bytes 1310752 | tf_op jit(solution)/shard_map/all_to_all | solution.py:151
  122.0 3.8 reduce.3
  125.8 62.1 %reshape.448 = f32[32768,2,5]{2,1,0:T(2,128)} reshape(f32[8,40960]{1,0:T(8,128)S(1)} %reduce.3) | data formatting | bytes 2621440
  187.9 26.8 %copy.73 = f32[2,5,8,4096]{3,2,0,1:T(8,128)S(1)} copy(f32[2,5,8,4096]{1,0,3,2:T(2,128)} %bitcast.262) | data formatting | bytes 2621440 | tf_op jit(solution)/shard_map/all_to_all | solution.py:151
  216.8 5.5 copy.51
  223.9 37.7 %psum.14 = f32[16,16]{1,0:T(8,128)S(1)} all-reduce(f32[16,16]{1,0:T(8,128)S(1)} %broadcast_select_fusion.1), channel_id=1, replica_groups=mesh['mem'=8,'lev'=4] {'mem','lev'}, use_global_device_ids=true, to_apply=%region_0.1 | all-reduce | flops 256 | bytes 2048 | tf_op jit(solution)/shard_map/psum | solution.py:156
  261.6 153.8 %while.56 = (s32[]{:T(128)}, f32[16,16]{1,0:T(8,128)S(1)}, f32[16,16]{1,0:T(8,128)S(1)}, f32[16]{0:T(128)S(1)}, f32[16,16]{1,0:T(8,128)S(1)}, /*index=5*/s32[16]...) while((s32[]{:T(128)}, f32[16,16]{1,0:T(8,128)S(1)}, ...), condition=%wide.region_5.6_spmd, body=%wide.region_1.5_spmd.sunk | while | flops 4271 | bytes 5831 | solution.py:78
  415.9 2.2 convolution_multiply_fusion.1
  418.3 118.7 %while.57 = (s32[]{:T(128)}, f32[16,5,4096]{2,1,0:T(8,128)S(1)}, s32[16]{0:T(128)S(1)}, f32[16,4096]{1,0:T(8,128)}, f32[16,5,4096]{2,0,1:T(8,128)}, /*index=5*/f...) while((s32[]{:T(128)}, f32[16,5,4096]{2,1,0:T(8,128)S(1)}, s32[16]{0:T(128)S(1)}, ...), condition=%wide.region_9.10_spmd, body=%wide.region_8.9_spmd.sunk | while | flops 3993605 | bytes 2687667 | solution.py:108
  537.0 3.3 fusion.97
  540.4 5.5 copy.57
  545.8 1.5 gather_fusion.1
  547.4 41.9 %psum.15 = f32[16,16]{1,0:T(8,128)S(1)} all-reduce(f32[16,16]{1,0:T(8,128)S(1)} %broadcast_select_fusion), channel_id=1, replica_groups=mesh['mem'=8,'lev'=4] {'mem','lev'}, use_global_device_ids=true, to_apply=%region_10.11 | all-reduce | flops 256 | bytes 2048 | tf_op jit(solution)/shard_map/psum | solution.py:156
  589.3 163.1 %while.58 = (s32[]{:T(128)}, f32[16,16]{1,0:T(8,128)S(1)}, f32[16,16]{1,0:T(8,128)S(1)}, f32[16]{0:T(128)S(1)}, f32[16,16]{1,0:T(8,128)S(1)}, /*index=5*/s32[16]...) while((s32[]{:T(128)}, f32[16,16]{1,0:T(8,128)S(1)}, ...), condition=%wide.region_15.16_spmd, body=%wide.region_11.15_spmd.sunk | while | flops 4271 | bytes 5831 | solution.py:78
  753.0 2.2 convolution_multiply_fusion
  755.9 120.0 %while.59 = (s32[]{:T(128)}, f32[16,5,4096]{2,1,0:T(8,128)S(1)}, s32[16]{0:T(128)S(1)}, f32[16,4096]{1,0:T(8,128)}, f32[16,5,4096]{2,0,1:T(8,128)}, /*index=5*/f...) while((s32[]{:T(128)}, f32[16,5,4096]{2,1,0:T(8,128)S(1)}, s32[16]{0:T(128)S(1)}, ...), condition=%wide.region_19.20_spmd, body=%wide.region_18.19_spmd.sunk | while | flops 3993605 | bytes 2687667 | solution.py:108
  875.9 1.9 convolution_add_fusion
  878.6 51.7 %all_to_all.33 = f32[16,5,4096]{2,1,0:T(8,128)S(1)} all-to-all(f32[16,5,4096]{2,1,0:T(8,128)S(1)} %copy.63), channel_id=1, replica_groups=mesh['mem'=8,'lev'=4] {'mem'}, dimensions={0} | all-to-all | bytes 2621440 | tf_op jit(solution)/shard_map/all_to_all | solution.py:166
  (677 shorter events, 318.5 us)
Async XLA Ops:
  1.0 1.7 copy-start.1
  1.0 1.7 copy-start.4
  82.7 7.7 copy-start.2
  82.7 8.7 copy-start.3
  82.7 8.8 copy-start.5
  82.7 8.8 copy-start.6
  82.7 38.8 %all-to-all-start = ((f32[8,1,40960]{2,1,0:T(1,128)}), f32[8,1,40960]{2,1,0:T(1,128)S(1)}, u32[]{:S(2)}, u32[]{:S(2)}) async-start(f32[8,1,40960]{2,1,0:T(1,128)} %reshape.447), calls=%async_computation | async-start | bytes 2621440 | tf_op jit(solution)/shard_map/all_to_all | solution.py:151
  216.8 199.1 %copy-start = (f32[16,5,4096]{2,0,1:T(8,128)}, f32[16,5,4096]{2,0,1:T(8,128)S(1)}, u32[]{:S(2)}) copy-start(f32[16,5,4096]{2,0,1:T(8,128)S(1)} %all_to_all.27) | copy-start | bytes 3932164
  540.3 49.0 %copy-start.7 = (f32[16]{0:T(128)S(1)}, f32[16]{0:T(128)}, u32[]{:S(2)}) copy-start(f32[16]{0:T(128)} %get-tuple-element.825) | copy-start | bytes 196
  540.4 49.0 %copy-start.8 = (f32[16]{0:T(128)S(1)}, f32[16]{0:T(128)}, u32[]{:S(2)}) copy-start(f32[16]{0:T(128)} %get-tuple-element.824) | copy-start | bytes 196
  752.4 0.6 copy-start.9
  755.3 0.7 copy-start.10
where the time goes:
time: 946 us; the launch traced here: 933 us
  local copies, waits for them, and re-layouts  358 us (38%)
  loops' own time  250 us (26%)
  blocking collectives  131 us (14%)
  other arithmetic  83.4 us (9%)
  matrix products  73.5 us (8%)
  waiting for transfers between devices  27.9 us (3%)
    another operation x2, loops' own time, obs_space(): prior_rows, obs_plan = lax.scan(advance_obs, prior_rows, positions)  189 us
    unnamed x24, local copies, waits for them, and re-layouts  116 us
    psum x2, blocking collectives, body(): prior_rows = lax.psum(partial_value, ('mem', 'lev'))  79.6 us
    another operation x2, loops' own time, settle(): weights, unused = lax.scan(solve_step, jnp.zeros_like(cross_cov), positions)  61.9 us
    all_to_all x1, blocking collectives, body(): lax.all_to_all(state_rows, 'mem', split_axis=0, concat_axis=2, tiled=True)  51.7 us
    dot_general x32, matrix products, solve_step(): jnp.einsum('j,jsc->sc', column, weights, precision=lax.Precision.HIGHEST)  46.1 us
    dynamic_slice x64, local copies, waits for them, and re-layouts, obs_space(): prior_rows, obs_plan = lax.scan(advance_obs, prior_rows, positions)  40.3 us
    dynamic_slice x32, local copies, waits for them, and re-layouts, solve_step(): lax.dynamic_index_in_dim(cross_cov, position, 0, False)  36.9 us
  transfers between devices with their start and end apart: 1, of which 1 were waited for; matrix products, arithmetic and copies ran while one was open for 0% of the time, Pallas kernels for 0%

commit v1 on v0

--- a/solution.py
+++ b/solution.py
@@ -2,10 +2,39 @@
 import jax.numpy as jnp
 from jax import lax
 from jax.sharding import PartitionSpec as P
+from jax.lax import axis_index, axis_size, ppermute
 
 NX = 512
 STEPS = 2
 LOC_HALF = 64
+
+
+def launch_the_thing(x_in, on_dim, x0):
+    r1 = x_in.shape
+    v_now = x_in.reshape(*r1[:on_dim], x0, r1[on_dim] // x0, *r1[on_dim + 1 :])
+    return jnp.moveaxis(v_now, on_dim, 0)
+
+
+def choose_object(local_x, along_dim):
+    local_x = jnp.moveaxis(local_x, 0, along_dim)
+    far_arr = local_x.shape
+    return local_x.reshape(
+        *far_arr[:along_dim], far_arr[along_dim] * far_arr[along_dim + 1], *far_arr[along_dim + 2 :]
+    )
+
+
+def surface_extend(payload, axis_tag, vals, packet):
+    a_next = axis_size(axis_tag)
+    tmp = axis_index(axis_tag)
+    carry, block_next = (a_next, tmp)
+    arr_now = launch_the_thing(payload, vals, carry)
+    slots = [arr_now[block_next]]
+    for tick in range(1, carry):
+        y1 = arr_now[block_next ^ tick]
+        f_now = ppermute(y1, axis_tag, [(pp, pp ^ tick) for pp in range(carry)])
+        slots.append(f_now)
+    arr_now = jnp.stack(slots)[block_next ^ jnp.arange(carry)]
+    return choose_object(arr_now, packet)
 
 
 def predicted_model_vector(
@@ -148,7 +177,7 @@
         gaspari_taper(grid_distance(obs_cells[batch_no], local_cells))
         for batch_no in range(batch_count)
     ]
-    state_rows = lax.all_to_all(by_cells, "mem", split_axis=2, concat_axis=0, tiled=True)
+    state_rows = surface_extend(by_cells, "mem", 2, packet=0)
     for batch_no in range(batch_count):
         partial_value = pick_rows(
             state_rows, obs_slabs[batch_no], obs_cells[batch_no], slab_base, cell_base

time: 946 us -> 768 us (0.81)
  local copies, waits for them, and re-layouts: 358 us -> 199 us
  waiting for transfers between devices: 27.9 us -> 14.4 us
    unnamed x24 -> x36, local copies, waits for them, and re-layouts: 116 us -> 2 us
    all_to_all x5 -> x0, local copies, waits for them, and re-layouts: 34.7 us -> none  [body(): lax.all_to_all(by_cells, 'mem', split_axis=2, concat_axis=0, tiled=True)]
    all_to_all x1 -> x0, waiting for transfers between devices: 27.9 us -> none  [body(): lax.all_to_all(by_cells, 'mem', split_axis=2, concat_axis=0, tiled=True)]
    reshape x1 -> x2, local copies, waits for them, and re-layouts: 22.3 us -> 7.66 us  [choose_object(): local_x.reshape(*far_arr[:along_dim], far_arr[along_dim] * far_arr[along_...]
    ppermute x0 -> x7, waiting for transfers between devices: none -> 14.4 us  [surface_extend(): f_now = ppermute(y1, axis_tag, [(pp, pp ^ tick) for pp in range(carry)])]
    ppermute x0 -> x7, starting transfers between devices: none -> 12.9 us  [surface_extend(): f_now = ppermute(y1, axis_tag, [(pp, pp ^ tick) for pp in range(carry)])]
  transfers between devices with their start and end apart: 1 -> 7, of which waited for: 1 -> 2; matrix products, arithmetic and copies ran while one was open for 0% -> 1% of each run, Pallas kernels for 0% -> 0%
where the time goes in v1:
time: 768 us; the launch traced here: 761 us
  loops' own time  246 us (32%)
  local copies, waits for them, and re-layouts  199 us (26%)
  blocking collectives  137 us (18%)
  other arithmetic  78.5 us (10%)
  matrix products  73.5 us (10%)
  waiting for transfers between devices  14.4 us (2%)
  starting transfers between devices  12.9 us (2%)
    another operation x2, loops' own time, obs_space(): prior_rows, obs_plan = lax.scan(advance_obs, prior_rows, positions)  187 us
    psum x2, blocking collectives, body(): prior_rows = lax.psum(partial_value, ('mem', 'lev'))  84.8 us
    another operation x2, loops' own time, settle(): weights, unused = lax.scan(solve_step, jnp.zeros_like(cross_cov), positions)  58.6 us
    all_to_all x1, blocking collectives, body(): lax.all_to_all(state_rows, 'mem', split_axis=0, concat_axis=2, tiled=True)  52.3 us
    dot_general x32, matrix products, solve_step(): jnp.einsum('j,jsc->sc', column, weights, precision=lax.Precision.HIGHEST)  46.1 us
    dynamic_slice x64, local copies, waits for them, and re-layouts, obs_space(): prior_rows, obs_plan = lax.scan(advance_obs, prior_rows, positions)  39.4 us
    dynamic_slice x32, local copies, waits for them, and re-layouts, solve_step(): lax.dynamic_index_in_dim(cross_cov, position, 0, False)  36.9 us
    dynamic_slice x32, local copies, waits for them, and re-layouts, solve_step(): taper_row = lax.dynamic_index_in_dim(cell_loc, position, 0, False)  29.6 us
  transfers between devices with their start and end apart: 7, of which 2 were waited for; matrix products, arithmetic and copies ran while one was open for 1% of the time, Pallas kernels for 0%

profile of v1, /device:TPU:0, one launch (start us, length us, event | category | flops | bytes accessed | tf_op | source)
XLA Modules:
  0.0 761.0 jit_solution(3414355131393233158)
XLA Ops:
  1.1 1.5 broadcast_multiply_fusion.2
  2.7 2.2 multiply_add_fusion.5
  5.0 2.2 multiply_add_fusion.4
  8.9 3.1 collective-permute-start
  12.1 1.6 collective-permute-start.1
  14.1 3.0 collective-permute-start.3
  19.6 1.6 fusion.55
  22.3 3.7 collective-permute-start.5
  26.4 14.1 %collective-permute-done.4 = f32[2,5,4096]{2,0,1:T(2,128)S(1)} collective-permute-done((f32[2,5,4096]{2,0,1:T(2,128)S(1)}, f32[2,5,4096]{2,0,1:T(2,128)S(1)}, u32[]{:S(2)}, u32[]{:S(2)}) %collective-permute-start.4) | collective-permute-done | bytes 163872 | tf_op jit(solution)/shard_map/ppermute | solution.py:34
  40.7 1.9 gather_fusion
  43.8 2.2 reshape.451
  46.0 5.5 copy.45
  53.0 45.2 %psum.14 = f32[16,16]{1,0:T(8,128)S(1)} all-reduce(f32[16,16]{1,0:T(8,128)S(1)} %broadcast_select_fusion.1), channel_id=1, replica_groups=mesh['mem'=8,'lev'=4] {'mem','lev'}, use_global_device_ids=true, to_apply=%region_0.1 | all-reduce | flops 256 | bytes 2048 | tf_op jit(solution)/shard_map/psum | solution.py:185
  98.3 152.7 %while.56 = (s32[]{:T(128)}, f32[16,16]{1,0:T(8,128)S(1)}, f32[16,16]{1,0:T(8,128)S(1)}, f32[16]{0:T(128)S(1)}, f32[16,16]{1,0:T(8,128)S(1)}, /*index=5*/s32[16]...) while((s32[]{:T(128)}, f32[16,16]{1,0:T(8,128)S(1)}, ...), condition=%wide.region_5.6_spmd, body=%wide.region_1.5_spmd.sunk | while | flops 4271 | bytes 5831 | solution.py:107
  252.0 2.2 convolution_multiply_fusion.1
  254.4 114.3 %while.57 = (s32[]{:T(128)}, f32[16,5,4096]{2,1,0:T(8,128)S(1)}, s32[16]{0:T(128)S(1)}, f32[16,4096]{1,0:T(8,128)}, f32[16,5,4096]{2,0,1:T(8,128)}, /*index=5*/f...) while((s32[]{:T(128)}, f32[16,5,4096]{2,1,0:T(8,128)S(1)}, s32[16]{0:T(128)S(1)}, ...), condition=%wide.region_9.10_spmd, body=%wide.region_8.9_spmd.sunk | while | flops 3993605 | bytes 2687667 | solution.py:137
  368.7 3.3 fusion.99
  372.1 5.5 copy.51
  379.1 39.6 %psum.15 = f32[16,16]{1,0:T(8,128)S(1)} all-reduce(f32[16,16]{1,0:T(8,128)S(1)} %broadcast_select_fusion), channel_id=1, replica_groups=mesh['mem'=8,'lev'=4] {'mem','lev'}, use_global_device_ids=true, to_apply=%region_10.11 | all-reduce | flops 256 | bytes 2048 | tf_op jit(solution)/shard_map/psum | solution.py:185
  418.7 163.1 %while.58 = (s32[]{:T(128)}, f32[16,16]{1,0:T(8,128)S(1)}, f32[16,16]{1,0:T(8,128)S(1)}, f32[16]{0:T(128)S(1)}, f32[16,16]{1,0:T(8,128)S(1)}, /*index=5*/s32[16]...) while((s32[]{:T(128)}, f32[16,16]{1,0:T(8,128)S(1)}, ...), condition=%wide.region_15.16_spmd, body=%wide.region_11.15_spmd.sunk | while | flops 4271 | bytes 5831 | solution.py:107
  582.4 2.2 convolution_multiply_fusion
  585.3 118.7 %while.59 = (s32[]{:T(128)}, f32[16,5,4096]{2,1,0:T(8,128)S(1)}, s32[16]{0:T(128)S(1)}, f32[16,4096]{1,0:T(8,128)}, f32[16,5,4096]{2,0,1:T(8,128)}, /*index=5*/f...) while((s32[]{:T(128)}, f32[16,5,4096]{2,1,0:T(8,128)S(1)}, s32[16]{0:T(128)S(1)}, ...), condition=%wide.region_19.20_spmd, body=%wide.region_18.19_spmd.sunk | while | flops 3993605 | bytes 2687667 | solution.py:137
  704.0 1.9 convolution_add_fusion
  706.7 52.3 %all_to_all.15 = f32[16,5,4096]{2,1,0:T(8,128)S(1)} all-to-all(f32[16,5,4096]{2,1,0:T(8,128)S(1)} %copy.57), channel_id=1, replica_groups=mesh['mem'=8,'lev'=4] {'mem'}, dimensions={0} | all-to-all | bytes 2621440 | tf_op jit(solution)/shard_map/all_to_all | solution.py:195
  (703 shorter events, 320.1 us)
Async XLA Ops:
  1.0 1.7 copy-start.1
  1.0 1.7 copy-start.4
  8.7 9.9 %copy-start.2 = (s32[2,16]{1,0:T(2,128)S(1)}, s32[2,16]{1,0:T(2,128)}, u32[]{:S(2)}) copy-start(s32[2,16]{1,0:T(2,128)} %param.20) | copy-start | bytes 388
  8.8 9.9 %copy-start.3 = (s32[2,16]{1,0:T(2,128)S(1)}, s32[2,16]{1,0:T(2,128)}, u32[]{:S(2)}) copy-start(s32[2,16]{1,0:T(2,128)} %param.21) | copy-start | bytes 388
  8.8 10.1 %copy-start.5 = (f32[2,16]{1,0:T(2,128)S(1)}, f32[2,16]{1,0:T(2,128)}, u32[]{:S(2)}) copy-start(f32[2,16]{1,0:T(2,128)} %param.22) | copy-start | bytes 388
  8.8 10.1 %copy-start.6 = (f32[2,16]{1,0:T(2,128)S(1)}, f32[2,16]{1,0:T(2,128)}, u32[]{:S(2)}) copy-start(f32[2,16]{1,0:T(2,128)} %param.23) | copy-start | bytes 388
  8.9 13.4 %collective-permute-start = (f32[2,5,4096]{2,0,1:T(2,128)S(1)}, f32[2,5,4096]{2,0,1:T(2,128)S(1)}, u32[]{:S(2)}, u32[]{:S(2)}) collective-permute-start(f32[2,5,4096]{2,0,1:T(2,128)S(1)} %bitcast.305), channel_id=1, source_target_pairs={{0,4},{4,0},{8,12},{12,8},{16,20},{20,16},{24,28},{28,24},{1,5},{5... | collective-permute-start | bytes 491528 | tf_op jit(solution)/shard_map/ppermute | solution.py:34
  12.1 13.9 %collective-permute-start.1 = (f32[2,5,4096]{2,0,1:T(2,128)S(1)}, f32[2,5,4096]{2,0,1:T(2,128)S(1)}, u32[]{:S(2)}, u32[]{:S(2)}) collective-permute-start(f32[2,5,4096]{2,0,1:T(2,128)S(1)} %bitcast.304), channel_id=1, source_target_pairs={{0,8},{4,12},{8,0},{12,4},{16,24},{20,28},{24,16},{28,20},{1,9},{5... | collective-permute-start | bytes 491528 | tf_op jit(solution)/shard_map/ppermute | solution.py:34
  13.9 12.5 %collective-permute-start.2 = (f32[2,5,4096]{2,0,1:T(2,128)S(1)}, f32[2,5,4096]{2,0,1:T(2,128)S(1)}, u32[]{:S(2)}, u32[]{:S(2)}) collective-permute-start(f32[2,5,4096]{2,0,1:T(2,128)S(1)} %bitcast.303), channel_id=1, source_target_pairs={{0,12},{4,8},{8,4},{12,0},{16,28},{20,24},{24,20},{28,16},{1,13},{... | collective-permute-start | bytes 491528 | tf_op jit(solution)/shard_map/ppermute | solution.py:34
  14.1 12.3 %collective-permute-start.3 = (f32[2,5,4096]{2,0,1:T(2,128)S(1)}, f32[2,5,4096]{2,0,1:T(2,128)S(1)}, u32[]{:S(2)}, u32[]{:S(2)}) collective-permute-start(f32[2,5,4096]{2,0,1:T(2,128)S(1)} %bitcast.302), channel_id=1, source_target_pairs={{0,16},{4,20},{8,24},{12,28},{16,0},{20,4},{24,8},{28,12},{1,17},{... | collective-permute-start | bytes 491528 | tf_op jit(solution)/shard_map/ppermute | solution.py:34
  17.3 23.3 %collective-permute-start.4 = (f32[2,5,4096]{2,0,1:T(2,128)S(1)}, f32[2,5,4096]{2,0,1:T(2,128)S(1)}, u32[]{:S(2)}, u32[]{:S(2)}) collective-permute-start(f32[2,5,4096]{2,0,1:T(2,128)S(1)} %bitcast.301), channel_id=1, source_target_pairs={{0,20},{4,16},{8,28},{12,24},{16,4},{20,0},{24,12},{28,8},{1,21},{... | collective-permute-start | bytes 491528 | tf_op jit(solution)/shard_map/ppermute | solution.py:34
  22.3 18.3 %collective-permute-start.5 = (f32[2,5,4096]{2,0,1:T(2,128)S(1)}, f32[2,5,4096]{2,0,1:T(2,128)S(1)}, u32[]{:S(2)}, u32[]{:S(2)}) collective-permute-start(f32[2,5,4096]{2,0,1:T(2,128)S(1)} %bitcast.307), channel_id=1, source_target_pairs={{0,24},{4,28},{8,16},{12,20},{16,8},{20,12},{24,0},{28,4},{1,25},{... | collective-permute-start | bytes 491528 | tf_op jit(solution)/shard_map/ppermute | solution.py:34
  26.0 14.6 %collective-permute-start.6 = (f32[2,5,4096]{2,0,1:T(2,128)S(1)}, f32[2,5,4096]{2,0,1:T(2,128)S(1)}, u32[]{:S(2)}, u32[]{:S(2)}) collective-permute-start(f32[2,5,4096]{2,0,1:T(2,128)S(1)} %bitcast.306), channel_id=1, source_target_pairs={{0,28},{4,24},{8,20},{12,16},{16,12},{20,8},{24,4},{28,0},{1,29},{... | collective-permute-start | bytes 491528 | tf_op jit(solution)/shard_map/ppermute | solution.py:34
  46.0 206.0 %copy-start = (f32[16,5,4096]{2,0,1:T(8,128)}, f32[16,5,4096]{2,0,1:T(8,128)S(1)}, u32[]{:S(2)}) copy-start(f32[16,5,4096]{2,0,1:T(8,128)S(1)} %reshape.451) | copy-start | bytes 3932164
  372.1 46.7 %copy-start.7 = (f32[16]{0:T(128)S(1)}, f32[16]{0:T(128)}, u32[]{:S(2)}) copy-start(f32[16]{0:T(128)} %get-tuple-element.801) | copy-start | bytes 196
  372.1 46.7 %copy-start.8 = (f32[16]{0:T(128)S(1)}, f32[16]{0:T(128)}, u32[]{:S(2)}) copy-start(f32[16]{0:T(128)} %get-tuple-element.800) | copy-start | bytes 196
  581.8 0.6 copy-start.9
  584.7 0.7 copy-start.10
